TPU v7x, 512 devices: a whole 4x4x16 slice. The times are simulated.
512 devices in a mesh: row: 16 (over z), col: 32 (over x, y, core).
Axes of the slice: x: 4, y: 4, z: 16, core: 2. Of those that a mesh axis runs over, the one named last changes fastest.
Arguments:
- operator_tiles: bfloat16 [64, 128, 9, 64, 64], P('row', 'col'), may hold values from -0.25 to 0.25
- neighbour_codes: int32 [64, 128, 9], P('row', 'col'), may hold values from 0 to 8, as said below
- live_slots: int32 [64, 128], P('row', 'col'), may hold values from 1 to 9, as said below
- prolong_tiles: bfloat16 [64, 128, 6, 64, 64], P('row', 'col'), may hold values from -0.75 to 0.75
- coarse_blocks: int32 [64, 128, 6], P('row', 'col'), may hold values from 0 to 127, as said below
Outputs:
- coarse_band: float32 [32, 256, 1792], P('col', 'row')
Inputs may be any that keep to these rules, and one draw needn't show every extreme that they name: `neighbour_codes`: A fine block's 9 codes differ; slot 0 holds 4, the block itself. Slots 0 to live_slots - 1 of a fine block are used; some fine block uses all 9. `coarse_blocks`: the 6 coarse blocks of a fine block in slab s differ and lie in slabs s - 1, s, s + 1 (mod 32); the first lies in slab s.
All inputs are finite; a program needn't handle non-finite values.
Results may differ from a plain program's by a relative error of at most 0.0029.
Values may be sent and summed in bfloat16 or wider, within the bound.
No kernel may reach another device: no remote copies, remote signals or barrier semaphores. Data moves between devices by JAX's collectives and lax.ppermute only.
A program may use at most 128 MiB of HBM per device.

v0:
```python
import jax
import jax.numpy as jnp
from jax import lax
from jax.experimental import pallas as pl
from jax.experimental.pallas import tpu as pltpu
from jax.sharding import PartitionSpec as P


B = 64
ROWS = 16
COLS = 32
F32 = jnp.float32
BF16 = jnp.bfloat16


def joint(rule):
    pairs = []
    for r in range(ROWS):
        for s in range(COLS):
            r2, s2 = rule(r, s)
            pairs.append((r * COLS + s, (r2 % ROWS) * COLS + s2 % COLS))
    return pairs


def send(value, rule):
    return lax.ppermute(value, ("row", "col"), joint(rule))


def sign(s):
    return 1 if s % 2 == 0 else -1


def smem():
    return pl.BlockSpec(memory_space=pltpu.SMEM)


def vmem():
    return pl.BlockSpec(memory_space=pltpu.VMEM)


def budget(mib, flops, moved):
    return dict(
        compiler_params=pltpu.CompilerParams(vmem_limit_bytes=mib << 20),
        cost_estimate=pl.CostEstimate(flops=flops, bytes_accessed=moved, transcendentals=0),
    )


PART4 = 4 * 192 + 4 * 16
PART6 = 6 * 192 + 6 * 16


def column_of(pos_ref, x, y, j):
    g = pos_ref[3 + (x * 4 + y) * 6 + j]
    return (((g >> 2) - pos_ref[2] + 33) & 31) * 4 + (g & 3)


def pack(pos_ref, p_ref, out_ref, n, x, y):
    for t in range(3):
        left = p_ref[(x * 4 + y) * 6 + 2 * t]
        right = p_ref[(x * 4 + y) * 6 + 2 * t + 1]
        at = 192 * n + 64 * t
        out_ref[at : at + 64, :] = jnp.concatenate([left, right], axis=1)
    row = lax.broadcasted_iota(jnp.int32, (16, 128), 0)
    table = jnp.zeros((16, 128), jnp.int32)
    for j in range(6):
        table = jnp.where(row == j, column_of(pos_ref, x, y, j), table)
    out_ref[768 + 16 * n : 784 + 16 * n, :] = table.astype(F32).astype(BF16)


def expand(message_ref, n, tables_at, store):
    tables = message_ref[pl.ds(pl.multiple_of(tables_at + 16 * n, 16), 16), :]
    tiles = []
    for t in range(3):
        pair = message_ref[pl.ds(pl.multiple_of(192 * n + 64 * t, 64), 64), :]
        left, right = pair[:, 0:64], pair[:, 64:128]
        tiles.append(jnp.concatenate([left, left], axis=1))
        tiles.append(jnp.concatenate([right, right], axis=1))
    spots = [jnp.broadcast_to(tables[j : j + 1, :], (64, 128)) for j in range(6)]
    spread(tiles, spots, store)


def spread(tiles, spots, store):
    odd = (lax.broadcasted_iota(jnp.int32, (64, 128), 1) // 64).astype(F32)
    for m in range(6):
        column = (odd + 2.0 * m).astype(BF16)
        out = jnp.zeros((64, 128), BF16)
        for j in range(6):
            out = jnp.where(spots[j] == column, tiles[j], out)
        store(slice(128 * m, 128 * m + 128), out)


def pack_kernel(pos_ref, p_ref, cross_ref, chip_ref):
    core = pos_ref[0]
    for x in range(4):
        pack(pos_ref, p_ref, cross_ref, x, x, core * 3)
        pack(pos_ref, p_ref, chip_ref, x, x, 3 - core * 3)


def packed(kernel, pos, tiles):
    return pl.pallas_call(
        kernel,
        out_shape=(jax.ShapeDtypeStruct((PART4, 128), BF16),) * 2,
        in_specs=[smem(), vmem()],
        out_specs=(vmem(),) * 2,
        **budget(4, 0, 2000000),
    )(pos, tiles)


def row_kernel(pos_ref, p_ref, up_ref, down_ref):
    for y in range(4):
        pack(pos_ref, p_ref, up_ref, y, 3, y)
        pack(pos_ref, p_ref, down_ref, y, 0, y)


def place_kernel(pos_ref, p_ref, po_ref):
    def block(b, carry):
        y, x = b >> 2, b & 3
        rows = pl.ds(pl.multiple_of(b * B, B), B)
        tiles = []
        spots = []
        for j in range(6):
            tile = p_ref[(x * 4 + y) * 6 + j]
            tiles.append(jnp.concatenate([tile, tile], axis=1))
            spots.append(jnp.full((64, 128), column_of(pos_ref, x, y, j).astype(F32)).astype(BF16))

        def store(cols, value):
            po_ref[rows, cols] = value

        spread(tiles, spots, store)
        return carry

    lax.fori_loop(0, 16, block, 0)


def place(pos, tiles):
    return pl.pallas_call(
        place_kernel,
        out_shape=jax.ShapeDtypeStruct((1024, 768), BF16),
        in_specs=[smem(), vmem()],
        out_specs=vmem(),
        name="place",
        **budget(4, 0, 2000000),
    )(pos, tiles)


def rim_kernel(up_own, down_own, cross_ref, chip_ref, up_ref, down_ref):
    for own, out, x in ((up_own, up_ref, 3), (down_own, down_ref, 0)):
        out[0:768, :] = own[0:768, :]
        out[1152:1216, :] = own[768:832, :]
        for n, ref in ((4, cross_ref), (5, chip_ref)):
            out[192 * n : 192 * n + 192, :] = ref[192 * x : 192 * x + 192, :]
            out[1152 + 16 * n : 1168 + 16 * n, :] = ref[768 + 16 * x : 784 + 16 * x, :]


def rims(*parts):
    return pl.pallas_call(
        rim_kernel,
        out_shape=(jax.ShapeDtypeStruct((PART6, 128), BF16),) * 2,
        in_specs=[vmem()] * 4,
        out_specs=(vmem(),) * 2,
        name="rims",
        **budget(4, 0, 2000000),
    )(*parts)


SLOTS = (
    ((1, 2), (None, None), (0, None)),
    ((0, 1), (2, None), (None, None)),
    ((None, 0), (1, 2), (None, None)),
    ((None, None), (0, 1), (None, 2)),
)


def dot(a, b):
    return jnp.dot(a, b, preferred_element_type=F32)


def local_kernel(
    pos_ref, codes_ref, live_ref, a_ref, po_ref, cross_ref, chip_ref,
    ad_ref, outer_ref, rest_ref, im_ref, side_ref, aidx_ref,
):
    core = pos_ref[0]
    r = pos_ref[1]

    def widen(x, carry):
        rows = pl.ds(pl.multiple_of(64 * x, 64), 64)
        for side, ref in ((core, cross_ref), (1 - core, chip_ref)):
            def store(cols, value):
                side_ref[side, rows, cols] = value

            expand(ref, x, 768, store)
        return carry

    lax.fori_loop(0, 4, widen, 0)

    def fill(b, carry):
        y = b >> 2
        at = b & 3
        for k in range(9):
            aidx_ref[codes_ref[at, y, k]] = jnp.where(k < live_ref[at, y], k, -1)

        def tile(x, c):
            if c is None:
                return jnp.zeros((B, B), BF16)
            k = aidx_ref[c]
            value = a_ref[(x * 4 + y) * 9 + jnp.maximum(k, 0)]
            return jnp.where(k >= 0, value, jnp.zeros_like(value))

        for x in range(4):
            @pl.when(at == x)
            def _():
                for dy in range(3):
                    for m in range(3):
                        left, right = SLOTS[x][m]
                        left = None if left is None else left * 3 + dy
                        right = None if right is None else right * 3 + dy
                        pair = jnp.concatenate([tile(x, left), tile(x, right)], axis=1)
                        lane = 256 * dy + 128 * m if m < 2 else 768 + 128 * dy
                        ad_ref[y, 64 * x : 64 * x + 64, lane : lane + 128] = pair
        return carry

    lax.fori_loop(0, 16, fill, 0)

    for y in range(4):
        first = 1 if y == 0 else 0
        last = 1 if y == 3 else 2
        im_ref[256 * y : 256 * y + 256, :] = dot(
            ad_ref[y, :, 256 * first : 256 * last + 256],
            po_ref[256 * (y + first - 1) : 256 * (y + last), :],
        )

    windows = ((core * 2, 1 - core), (1 + core * 0, core), (2 - core * 2, 1 - core))
    for n, (window, kind) in enumerate(windows):
        lanes = pl.ds(pl.multiple_of(window * 256, 256), 256)
        for y in range(4):
            flipped = po_ref[256 * y : 256 * y + 256, lanes].T
            for o in range(16):
                shifted = (o - r - kind + 32) & 15
                flow = shifted >> 3
                near = jnp.where(flow == 0, shifted, 15 - shifted)
                half = (flow + core) & 1
                spot = half * 8 + (near & 1) * 4 + (near & 2) + (near >> 2)
                row = pl.multiple_of(max(n - 1, 0) * 256 + spot * 16, 16)
                pt_ref = rest_ref if n else outer_ref
                pt_ref[pl.ds(row, 16), 256 * y : 256 * y + 256] = flipped[16 * o : 16 * o + 16, :]


def local_products(pos, codes, live, a, po, cross, chip):
    return pl.pallas_call(
        local_kernel,
        out_shape=(
            jax.ShapeDtypeStruct((4, 256, 1152), BF16),
            jax.ShapeDtypeStruct((256, 1024), BF16),
            jax.ShapeDtypeStruct((512, 1024), BF16),
            jax.ShapeDtypeStruct((1024, 768), F32),
            jax.ShapeDtypeStruct((2, 256, 768), BF16),
        ),
        in_specs=[smem(), smem(), smem()] + [vmem()] * 4,
        out_specs=(vmem(),) * 5,
        scratch_shapes=[pltpu.SMEM((9,), jnp.int32)],
        name="local_products",
        **budget(12, 1000000000, 12000000),
    )(pos, codes, live, a, po, cross, chip)


def pieces(pt_ref, base, im_ref, store):
    for chunk in range(5):
        k = slice(0, 256) if chunk == 0 else slice(768, 1024) if chunk == 4 else slice(0, 1024)
        cols = slice(256 * chunk, 256 * chunk + 256)
        store(cols, dot(pt_ref[base : base + 256, k], im_ref[k, cols]))


def halo_kernel(
    pos_ref, ad_ref, pt_ref, part_ref, side_ref, up_ref, down_ref,
    im_ref, same_ref, other_ref, hr_ref,
):
    core = pos_ref[0]

    def widen(n, carry):
        to = jnp.where(n < 4, n + 1, jnp.where(n == 4, core * 5, 5 - core * 5))
        for at, ref in ((0, up_ref), (64, down_ref)):
            def store(cols, value):
                hr_ref[to, at : at + 64, cols] = value

            expand(ref, n, 1152, store)
        return carry

    lax.fori_loop(0, 6, widen, 0)

    for y in range(4):
        rows = slice(256 * y, 256 * y + 256)
        first = 1 if y == 0 else 0
        last = 1 if y == 3 else 2
        count = last - first + 1
        total = part_ref[rows, :] + dot(
            ad_ref[y, :, 768 + 128 * first : 896 + 128 * last],
            hr_ref[y + first : y + last + 1].reshape(128 * count, 768),
        )
        if count == 3:
            im_ref[rows, 256:1024] = total.astype(BF16)
            continue
        dy, side, at = (0, 0, 0) if y == 0 else (2, 1, 5)
        edge = dot(ad_ref[y, :, 256 * dy : 256 * dy + 256], side_ref[side])
        edge = edge + dot(ad_ref[y, :, 768 + 128 * dy : 896 + 128 * dy], hr_ref[at])
        if y == 0:
            im_ref[rows, 0:256] = edge[:, 0:256].astype(BF16)
            im_ref[rows, 256:768] = (edge[:, 256:768] + total[:, 0:512]).astype(BF16)
            im_ref[rows, 768:1024] = total[:, 512:768].astype(BF16)
        else:
            im_ref[rows, 256:512] = total[:, 0:256].astype(BF16)
            im_ref[rows, 512:1024] = (edge[:, 0:512] + total[:, 256:768]).astype(BF16)
            im_ref[rows, 1024:1280] = edge[:, 512:768].astype(BF16)

    def store(cols, out):
        same_ref[:, cols] = out[0:128].astype(BF16)
        other_ref[:, cols] = out[128:256].astype(BF16)

    pieces(pt_ref, 0, im_ref, store)


def halo_products(pos, ad, pt, part, *halo):
    half = jax.ShapeDtypeStruct((128, 1280), BF16)
    return pl.pallas_call(
        halo_kernel,
        out_shape=(jax.ShapeDtypeStruct((1024, 1280), BF16), half, half),
        in_specs=[smem()] + [vmem()] * 6,
        out_specs=(vmem(),) * 3,
        scratch_shapes=[pltpu.VMEM((6, 128, 768), BF16)],
        name="halo_products",
        **budget(12, 1500000000, 12000000),
    )(pos, ad, pt, part, *halo)


def own_kernel(pt_ref, im_ref, keep_ref, swap_ref):
    for n in range(2):
        def store(cols, out):
            keep_ref[128 * n : 128 * n + 128, cols] = out[0:128]
            swap_ref[128 * n : 128 * n + 128, cols] = out[128:256].astype(BF16)

        pieces(pt_ref, 256 * n, im_ref, store)


def own_pieces(pt, im):
    return pl.pallas_call(
        own_kernel,
        out_shape=(
            jax.ShapeDtypeStruct((256, 1280), F32),
            jax.ShapeDtypeStruct((256, 1280), BF16),
        ),
        in_specs=[vmem(), vmem()],
        out_specs=(vmem(), vmem()),
        name="own_pieces",
        **budget(8, 1400000000, 6000000),
    )(pt, im)


def merge_kernel(pos_ref, low_ref, middle_ref, high_ref, out_ref, sum_ref):
    zero = jnp.zeros((64, 256), F32)
    for at in (0, 1536):
        sum_ref[:, at : at + 256] = zero
    sum_ref[:, 256:1536] = middle_ref[...].astype(F32)

    def add(low, high):
        sum_ref[:, 0:1280] += low[...].astype(F32)
        sum_ref[:, 512:1792] += high[...].astype(F32)

    @pl.when(pos_ref[0] == 0)
    def _():
        add(low_ref, high_ref)

    @pl.when(pos_ref[0] == 1)
    def _():
        add(high_ref, low_ref)

    out_ref[...] = sum_ref[...].astype(out_ref.dtype)


def merged(pos, low, middle, high, dtype):
    parts = (low, middle, high)

    def rows(at):
        return pl.BlockSpec((64, 1280), lambda i: (at, 0))

    return pl.pallas_call(
        merge_kernel,
        grid=(1,),
        out_shape=jax.ShapeDtypeStruct((64, 1792), dtype),
        in_specs=[smem()] + [rows(at) for _, at in parts],
        out_specs=pl.BlockSpec((64, 1792), lambda i: (0, 0)),
        scratch_shapes=[pltpu.VMEM((64, 1792), F32)],
        **budget(4, 0, 1000000),
    )(pos, *(array for array, _ in parts))


def body(operator_tiles, neighbour_codes, live_slots, prolong_tiles, coarse_blocks):
    r = lax.axis_index("row")
    s = lax.axis_index("col")
    core = s % 2
    pos = jnp.concatenate([jnp.stack([core, r, s]).astype(jnp.int32), coarse_blocks.reshape(96)])

    tiles = prolong_tiles.reshape(96, B, B)
    cross, chip = packed(pack_kernel, pos, tiles)
    cross_in = send(cross, lambda r, s: (r, s - sign(s)))
    chip_in = send(chip, lambda r, s: (r, s + sign(s)))
    up_own, down_own = packed(row_kernel, pos, tiles)
    up, down = rims(up_own, down_own, cross_in, chip_in)
    up_in = send(up, lambda r, s: (r + 1, s))
    down_in = send(down, lambda r, s: (r - 1, s))
    po = place(pos, tiles)
    ad, outer, rest, part, side = local_products(
        pos, neighbour_codes, live_slots, operator_tiles.reshape(144, B, B), po, cross_in, chip_in
    )
    im, same, other = halo_products(pos, ad, outer, part, side, up_in, down_in)
    other_in = send(other, lambda r, s: (r, s - sign(s)))
    same_in = send(same, lambda r, s: (r, s - 2 * sign(s)))
    keep, swap = own_pieces(rest, im)
    swap_in = send(swap, lambda r, s: (r, s + sign(s)))
    other_slab = ((keep, 2), (swap_in, 0), (same_in, 0))
    own_slab = ((other_in, 0), (keep, 0), (swap_in, 2))

    def later(parts):
        return tuple((array, at + 1) for array, at in parts)

    def hop(step, value):
        return send(value, lambda r, s: (r + step * sign(s), s)).astype(F32)

    first = {}
    kept = {}
    for label, parts in (("p", other_slab), ("o", own_slab)):
        first[label] = hop(1, merged(pos, *later(parts), BF16))
    for label, parts in (("p", other_slab), ("o", own_slab)):
        kept[label] = merged(pos, *parts, F32)
    total = {}
    for label in ("p", "o"):
        got = first[label]
        acc = kept[label]
        for step, size in ((2, 32), (4, 16)):
            moved = hop(step, (acc[size:] + got[size:]).astype(BF16))
            acc = acc[:size] + got[:size]
            got = moved
        total[label] = acc + got
    last = send(total["p"], lambda r, s: (r + sign(s), s + sign(s)))
    return (total["o"] + last)[None]


def solution(mesh):
    in_specs = (
        P("row", "col", None, None, None),
        P("row", "col", None),
        P("row", "col"),
        P("row", "col", None, None, None),
        P("row", "col", None),
    )
    out_specs = P("col", "row", None)
    return jax.shard_map(
        body, mesh=mesh, in_specs=in_specs, out_specs=out_specs, check_vma=False
    )
```

profile of v0, /device:TPU:1, one launch (start us, length us, event | category | flops | bytes accessed | tf_op | source)
XLA Modules:
  0.0 97.9 jit_solution(7449786204567024790)
XLA Ops:
  0.0 0.8 reshape.9
  0.8 0.1 pad_add_fusion.pos_ref
  0.9 1.4 %copy-done = bf16[4,4,6,64,64]{4,3,2,1,0:T(8,128)(2,1)S(1)} copy-done((bf16[4,4,6,64,64]{4,3,2,1,0:T(8,128)(2,1)S(1)}, bf16[4,4,6,64,64]{4,3,2,1,0:T(8,128)(2,1)}, u32[]{:S(2)}) %copy-start) | copy-done | bytes 786456
  2.3 0.7 shard_map.55
  3.0 4.6 %collective-permute-start = (bf16[832,128]{1,0:T(8,128)(2,1)S(1)}, bf16[832,128]{1,0:T(8,128)(2,1)S(1)}, u32[]{:S(2)}, u32[]{:S(2)}) collective-permute-start(bf16[832,128]{1,0:T(8,128)(2,1)S(1)} %get-tuple-element.21), channel_id=1, source_target_pairs={{0,31},{1,2},{2,1},{3,4},{4,3},{5,6},{6,5},{7,8},{8,7},{9,10},{10,... | collective-permute-start | bytes 638984 | tf_op jit(solution)/shard_map/ppermute | solution.py:26
  7.6 6.1 %collective-permute-start.1 = (bf16[832,128]{1,0:T(8,128)(2,1)S(1)}, bf16[832,128]{1,0:T(8,128)(2,1)S(1)}, u32[]{:S(2)}, u32[]{:S(2)}) collective-permute-start(bf16[832,128]{1,0:T(8,128)(2,1)S(1)} %get-tuple-element.22), channel_id=1, source_target_pairs={{0,1},{1,0},{2,3},{3,2},{4,5},{5,4},{6,7},{7,6},{8,9},{9,8},{10,11... | collective-permute-start | bytes 638984 | tf_op jit(solution)/shard_map/ppermute | solution.py:26
  13.7 0.7 shard_map.56
  14.5 0.0 copy-start.2
  14.5 0.0 copy-start.3
  14.5 0.0 copy-start.4
  14.5 0.0 collective-permute-done.cross_ref
  14.5 0.3 collective-permute-done.1.chip_ref
  14.8 3.0 %collective-permute-start.2 = (bf16[1248,128]{1,0:T(8,128)(2,1)S(1)}, bf16[1248,128]{1,0:T(8,128)(2,1)S(1)}, u32[]{:S(2)}, u32[]{:S(2)}) collective-permute-start(bf16[1248,128]{1,0:T(8,128)(2,1)S(1)} %get-tuple-element.29), channel_id=1, source_target_pairs={{0,32},{1,33},{2,34},{3,35},{4,36},{5,37},{6,38},{7,39},{8,40},{9,... | collective-permute-start | bytes 958472 | tf_op jit(solution)/shard_map/ppermute | solution.py:26
  17.8 9.5 %collective-permute-start.3 = (bf16[1248,128]{1,0:T(8,128)(2,1)S(1)}, bf16[1248,128]{1,0:T(8,128)(2,1)S(1)}, u32[]{:S(2)}, u32[]{:S(2)}) collective-permute-start(bf16[1248,128]{1,0:T(8,128)(2,1)S(1)} %get-tuple-element.30), channel_id=1, source_target_pairs={{0,480},{1,481},{2,482},{3,483},{4,484},{5,485},{6,486},{7,487},{8... | collective-permute-start | bytes 958472 | tf_op jit(solution)/shard_map/ppermute | solution.py:26
  27.3 2.3 %place.1.po_ref = bf16[1024,768]{1,0:T(8,128)(2,1)S(1)} custom-call(s32[99]{0:T(128)S(1)} %pad_add_fusion.pos_ref, bf16[96,64,64]{2,1,0:T(8,128)(2,1)S(1)} %bitcast.9), custom_call_target="tpu_custom_call" | custom-call | bytes 2000000 | tf_op jit(solution)/shard_map/place/pallas_call | solution.py:136
  29.6 0.0 copy-done.2
  29.6 4.8 %local_products.1 = (bf16[4,256,1152]{2,1,0:T(8,128)(2,1)S(1)}, bf16[256,1024]{1,0:T(8,128)(2,1)S(1)}, bf16[512,1024]{1,0:T(8,128)(2,1)S(1)}, f32[1024,768]{1,0:T(8,128)S(1)}, bf16[2,256,768]{2,1,0:T(8,128)(2,1)S(1)}) custom-call(s32[99]{0:T(128)S(1)} %pad_add_fusion.pos_ref, s32[4,4,9]{2,1,0:T(4,128)S(1)} %copy-done.3, s32[4,4]{1,0:T(4,128)S(1)} %copy-done.4, ...), custom_call_target="tpu_custom_call" | custom-call | flops 1000000000 | bytes 12000000 | tf_op jit(solution)/shard_map/local_products/pallas_call | solution.py:249
  34.4 0.0 collective-permute-done.2.up_ref
  34.4 0.0 collective-permute-done.3.down_ref
  34.4 3.1 %halo_products.1 = (bf16[1024,1280]{1,0:T(8,128)(2,1)S(1)}, bf16[128,1280]{1,0:T(8,128)(2,1)S(1)}, bf16[128,1280]{1,0:T(8,128)(2,1)S(1)}) custom-call(s32[99]{0:T(128)S(1)} %pad_add_fusion.pos_ref, bf16[4,256,1152]{2,1,0:T(8,128)(2,1)S(1)} %get-tuple-element.23.ad_ref, bf16[256,1024]{1,0:T(8,128)(2,1)S(1)} %get-tuple-element.24.pt_ref, ...), custom_call_target="tpu_custom_call" | custom-call | flops 1500000000 | bytes 12000000 | tf_op jit(solution)/shard_map/halo_products/pallas_call | solution.py:323
  37.6 1.1 %own_pieces.1 = (f32[256,1280]{1,0:T(8,128)S(1)}, bf16[256,1280]{1,0:T(8,128)(2,1)S(1)}) custom-call(bf16[512,1024]{1,0:T(8,128)(2,1)S(1)} %get-tuple-element.32.pt_ref, bf16[1024,1280]{1,0:T(8,128)(2,1)S(1)} %get-tuple-element.33.im_ref), custom_call_target="tpu_custom_call" | custom-call | flops 1400000000 | bytes 6000000 | tf_op jit(solution)/shard_map/own_pieces/pallas_call | solution.py:344
  38.7 3.0 %collective-permute-start.5 = (bf16[256,1280]{1,0:T(8,128)(2,1)S(1)}, bf16[256,1280]{1,0:T(8,128)(2,1)S(1)}, u32[]{:S(2)}, u32[]{:S(2)}) collective-permute-start(bf16[256,1280]{1,0:T(8,128)(2,1)S(1)} %get-tuple-element.35), channel_id=1, source_target_pairs={{0,1},{1,0},{2,3},{3,2},{4,5},{5,4},{6,7},{7,6},{8,9},{9,8},{10,11... | collective-permute-start | bytes 1966088 | tf_op jit(solution)/shard_map/ppermute | solution.py:26
  41.7 1.9 %collective-permute-start.9 = (bf16[128,1280]{1,0:T(8,128)(2,1)S(1)}, bf16[128,1280]{1,0:T(8,128)(2,1)S(1)}, u32[]{:S(2)}, u32[]{:S(2)}) collective-permute-start(bf16[128,1280]{1,0:T(8,128)(2,1)S(1)} %get-tuple-element.36), channel_id=1, source_target_pairs={{0,30},{1,3},{2,0},{3,5},{4,2},{5,7},{6,4},{7,9},{8,6},{9,11},{10,... | collective-permute-start | bytes 983048 | tf_op jit(solution)/shard_map/ppermute | solution.py:26
  43.6 3.5 %collective-permute-start.4 = (bf16[128,1280]{1,0:T(8,128)(2,1)S(1)}, bf16[128,1280]{1,0:T(8,128)(2,1)S(1)}, u32[]{:S(2)}, u32[]{:S(2)}) collective-permute-start(bf16[128,1280]{1,0:T(8,128)(2,1)S(1)} %get-tuple-element.31), channel_id=1, source_target_pairs={{0,31},{1,2},{2,1},{3,4},{4,3},{5,6},{6,5},{7,8},{8,7},{9,10},{10,... | collective-permute-start | bytes 983048 | tf_op jit(solution)/shard_map/ppermute | solution.py:26
  47.2 5.7 %collective-permute-done.9.high_ref = bf16[128,1280]{1,0:T(8,128)(2,1)S(1)} collective-permute-done((bf16[128,1280]{1,0:T(8,128)(2,1)S(1)}, bf16[128,1280]{1,0:T(8,128)(2,1)S(1)}, u32[]{:S(2)}, u32[]{:S(2)}) %collective-permute-start.9) | collective-permute-done | bytes 327712 | tf_op jit(solution)/shard_map/ppermute | solution.py:26
  52.8 0.0 collective-permute-done.5.high_ref.middle_ref
  52.9 0.7 shard_map.60
  53.5 4.8 %collective-permute-start.10 = (bf16[64,1792]{1,0:T(8,128)(2,1)S(1)}, bf16[64,1792]{1,0:T(8,128)(2,1)S(1)}, u32[]{:S(2)}, u32[]{:S(2)}) collective-permute-start(bf16[64,1792]{1,0:T(8,128)(2,1)S(1)} %shard_map.60), channel_id=1, source_target_pairs={{0,32},{1,481},{2,34},{3,483},{4,36},{5,485},{6,38},{7,487},{8,40}... | collective-permute-start | bytes 688136 | tf_op jit(solution)/shard_map/ppermute | solution.py:26
  58.4 0.0 collective-permute-done.4.low_ref
  58.4 0.7 shard_map.58
  59.1 2.2 %collective-permute-start.6 = (bf16[64,1792]{1,0:T(8,128)(2,1)S(1)}, bf16[64,1792]{1,0:T(8,128)(2,1)S(1)}, u32[]{:S(2)}, u32[]{:S(2)}) collective-permute-start(bf16[64,1792]{1,0:T(8,128)(2,1)S(1)} %shard_map.58), channel_id=1, source_target_pairs={{0,32},{1,481},{2,34},{3,483},{4,36},{5,485},{6,38},{7,487},{8,40}... | collective-permute-start | bytes 688136 | tf_op jit(solution)/shard_map/ppermute | solution.py:26
  61.2 0.7 shard_map.59
  61.9 0.7 shard_map.57
  62.6 0.0 collective-permute-done.10
  62.6 0.1 slice_add_fusion.1
  62.7 3.6 %collective-permute-start.11 = (bf16[32,1792]{1,0:T(8,128)(2,1)S(1)}, bf16[32,1792]{1,0:T(8,128)(2,1)S(1)}, u32[]{:S(2)}, u32[]{:S(2)}) collective-permute-start(bf16[32,1792]{1,0:T(8,128)(2,1)S(1)} %get-tuple-element.40), channel_id=1, source_target_pairs={{0,64},{1,449},{2,66},{3,451},{4,68},{5,453},{6,70},{7,455},{8,72}... | collective-permute-start | bytes 344072 | tf_op jit(solution)/shard_map/ppermute | solution.py:26
  66.3 0.0 collective-permute-done.6
  66.3 0.1 slice_add_fusion.3
  66.4 4.3 %collective-permute-start.7 = (bf16[32,1792]{1,0:T(8,128)(2,1)S(1)}, bf16[32,1792]{1,0:T(8,128)(2,1)S(1)}, u32[]{:S(2)}, u32[]{:S(2)}) collective-permute-start(bf16[32,1792]{1,0:T(8,128)(2,1)S(1)} %get-tuple-element.38), channel_id=1, source_target_pairs={{0,64},{1,449},{2,66},{3,451},{4,68},{5,453},{6,70},{7,455},{8,72}... | collective-permute-start | bytes 344072 | tf_op jit(solution)/shard_map/ppermute | solution.py:26
  70.7 0.0 collective-permute-done.11
  70.8 5.2 %collective-permute-start.12 = (bf16[16,1792]{1,0:T(8,128)(2,1)S(1)}, bf16[16,1792]{1,0:T(8,128)(2,1)S(1)}, u32[]{:S(2)}, u32[]{:S(2)}) collective-permute-start(bf16[16,1792]{1,0:T(8,128)(2,1)S(1)} %fusion.2), channel_id=1, source_target_pairs={{0,128},{1,385},{2,130},{3,387},{4,132},{5,389},{6,134},{7,391},{8... | collective-permute-start | bytes 172040 | tf_op jit(solution)/shard_map/ppermute | solution.py:26
  75.9 0.0 collective-permute-done.7
  76.0 4.5 %collective-permute-done.12 = bf16[16,1792]{1,0:T(8,128)(2,1)S(1)} collective-permute-done((bf16[16,1792]{1,0:T(8,128)(2,1)S(1)}, bf16[16,1792]{1,0:T(8,128)(2,1)S(1)}, u32[]{:S(2)}, u32[]{:S(2)}) %collective-permute-start.12) | collective-permute-done | bytes 57376 | tf_op jit(solution)/shard_map/ppermute | solution.py:26
  80.5 7.7 %collective-permute-start.13 = (f32[16,1792]{1,0:T(8,128)S(1)}, f32[16,1792]{1,0:T(8,128)S(1)}, u32[]{:S(2)}, u32[]{:S(2)}) collective-permute-start(f32[16,1792]{1,0:T(8,128)S(1)} %fusion.3), channel_id=1, source_target_pairs={{0,33},{1,480},{2,35},{3,482},{4,37},{5,484},{6,39},{7,486},{8,41}... | collective-permute-start | bytes 344072 | tf_op jit(solution)/shard_map/ppermute | solution.py:26
  88.3 7.1 %collective-permute-start.8 = (bf16[16,1792]{1,0:T(8,128)(2,1)S(1)}, bf16[16,1792]{1,0:T(8,128)(2,1)S(1)}, u32[]{:S(2)}, u32[]{:S(2)}) collective-permute-start(bf16[16,1792]{1,0:T(8,128)(2,1)S(1)} %fusion.4), channel_id=1, source_target_pairs={{0,128},{1,385},{2,130},{3,387},{4,132},{5,389},{6,134},{7,391},{8... | collective-permute-start | bytes 172040 | tf_op jit(solution)/shard_map/ppermute | solution.py:26
  95.4 1.8 %collective-permute-done.8 = bf16[16,1792]{1,0:T(8,128)(2,1)S(1)} collective-permute-done((bf16[16,1792]{1,0:T(8,128)(2,1)S(1)}, bf16[16,1792]{1,0:T(8,128)(2,1)S(1)}, u32[]{:S(2)}, u32[]{:S(2)}) %collective-permute-start.8) | collective-permute-done | bytes 57376 | tf_op jit(solution)/shard_map/ppermute | solution.py:26
  97.2 0.0 collective-permute-done.13
  97.2 0.7 fusion.7
  (13 shorter events, 0.2 us)
Async XLA Ops:
  0.9 1.4 %copy-start = (bf16[4,4,6,64,64]{4,3,2,1,0:T(8,128)(2,1)S(1)}, bf16[4,4,6,64,64]{4,3,2,1,0:T(8,128)(2,1)}, u32[]{:S(2)}) copy-start(bf16[4,4,6,64,64]{4,3,2,1,0:T(8,128)(2,1)} %param.8) | copy-start | bytes 2359300
  2.3 25.0 %copy-start.1 = (bf16[4,4,6,64,64]{4,3,2,1,0:T(8,128)(2,1)S(1)}, bf16[4,4,6,64,64]{4,3,2,1,0:T(8,128)(2,1)}, u32[]{:S(2)}) copy-start(bf16[4,4,6,64,64]{4,3,2,1,0:T(8,128)(2,1)} %param.8) | copy-start | bytes 2359300
  3.0 11.5 %collective-permute-start = (bf16[832,128]{1,0:T(8,128)(2,1)S(1)}, bf16[832,128]{1,0:T(8,128)(2,1)S(1)}, u32[]{:S(2)}, u32[]{:S(2)}) collective-permute-start(bf16[832,128]{1,0:T(8,128)(2,1)S(1)} %get-tuple-element.21), channel_id=1, source_target_pairs={{0,31},{1,2},{2,1},{3,4},{4,3},{5,6},{6,5},{7,8},{8,7},{9,10},{10,... | collective-permute-start | bytes 638984 | tf_op jit(solution)/shard_map/ppermute | solution.py:26
  7.6 7.2 %collective-permute-start.1 = (bf16[832,128]{1,0:T(8,128)(2,1)S(1)}, bf16[832,128]{1,0:T(8,128)(2,1)S(1)}, u32[]{:S(2)}, u32[]{:S(2)}) collective-permute-start(bf16[832,128]{1,0:T(8,128)(2,1)S(1)} %get-tuple-element.22), channel_id=1, source_target_pairs={{0,1},{1,0},{2,3},{3,2},{4,5},{5,4},{6,7},{7,6},{8,9},{9,8},{10,11... | collective-permute-start | bytes 638984 | tf_op jit(solution)/shard_map/ppermute | solution.py:26
  14.5 15.1 %copy-start.2 = (bf16[4,4,9,64,64]{4,3,2,1,0:T(8,128)(2,1)S(1)}, bf16[4,4,9,64,64]{4,3,2,1,0:T(8,128)(2,1)}, u32[]{:S(2)}) copy-start(bf16[4,4,9,64,64]{4,3,2,1,0:T(8,128)(2,1)} %param.5) | copy-start | bytes 3538948
  14.5 15.1 %copy-start.3 = (s32[4,4,9]{2,1,0:T(4,128)S(1)}, s32[4,4,9]{2,1,0:T(4,128)}, u32[]{:S(2)}) copy-start(s32[4,4,9]{2,1,0:T(4,128)} %codes_ref.1) | copy-start | bytes 1732
  14.5 15.1 %copy-start.4 = (s32[4,4]{1,0:T(4,128)S(1)}, s32[4,4]{1,0:T(4,128)}, u32[]{:S(2)}) copy-start(s32[4,4]{1,0:T(4,128)} %live_ref.1) | copy-start | bytes 196
  14.8 19.6 %collective-permute-start.2 = (bf16[1248,128]{1,0:T(8,128)(2,1)S(1)}, bf16[1248,128]{1,0:T(8,128)(2,1)S(1)}, u32[]{:S(2)}, u32[]{:S(2)}) collective-permute-start(bf16[1248,128]{1,0:T(8,128)(2,1)S(1)} %get-tuple-element.29), channel_id=1, source_target_pairs={{0,32},{1,33},{2,34},{3,35},{4,36},{5,37},{6,38},{7,39},{8,40},{9,... | collective-permute-start | bytes 958472 | tf_op jit(solution)/shard_map/ppermute | solution.py:26
  17.8 16.6 %collective-permute-start.3 = (bf16[1248,128]{1,0:T(8,128)(2,1)S(1)}, bf16[1248,128]{1,0:T(8,128)(2,1)S(1)}, u32[]{:S(2)}, u32[]{:S(2)}) collective-permute-start(bf16[1248,128]{1,0:T(8,128)(2,1)S(1)} %get-tuple-element.30), channel_id=1, source_target_pairs={{0,480},{1,481},{2,482},{3,483},{4,484},{5,485},{6,486},{7,487},{8... | collective-permute-start | bytes 958472 | tf_op jit(solution)/shard_map/ppermute | solution.py:26
  38.7 14.1 %collective-permute-start.5 = (bf16[256,1280]{1,0:T(8,128)(2,1)S(1)}, bf16[256,1280]{1,0:T(8,128)(2,1)S(1)}, u32[]{:S(2)}, u32[]{:S(2)}) collective-permute-start(bf16[256,1280]{1,0:T(8,128)(2,1)S(1)} %get-tuple-element.35), channel_id=1, source_target_pairs={{0,1},{1,0},{2,3},{3,2},{4,5},{5,4},{6,7},{7,6},{8,9},{9,8},{10,11... | collective-permute-start | bytes 1966088 | tf_op jit(solution)/shard_map/ppermute | solution.py:26
  41.7 11.1 %collective-permute-start.9 = (bf16[128,1280]{1,0:T(8,128)(2,1)S(1)}, bf16[128,1280]{1,0:T(8,128)(2,1)S(1)}, u32[]{:S(2)}, u32[]{:S(2)}) collective-permute-start(bf16[128,1280]{1,0:T(8,128)(2,1)S(1)} %get-tuple-element.36), channel_id=1, source_target_pairs={{0,30},{1,3},{2,0},{3,5},{4,2},{5,7},{6,4},{7,9},{8,6},{9,11},{10,... | collective-permute-start | bytes 983048 | tf_op jit(solution)/shard_map/ppermute | solution.py:26
  43.6 14.7 %collective-permute-start.4 = (bf16[128,1280]{1,0:T(8,128)(2,1)S(1)}, bf16[128,1280]{1,0:T(8,128)(2,1)S(1)}, u32[]{:S(2)}, u32[]{:S(2)}) collective-permute-start(bf16[128,1280]{1,0:T(8,128)(2,1)S(1)} %get-tuple-element.31), channel_id=1, source_target_pairs={{0,31},{1,2},{2,1},{3,4},{4,3},{5,6},{6,5},{7,8},{8,7},{9,10},{10,... | collective-permute-start | bytes 983048 | tf_op jit(solution)/shard_map/ppermute | solution.py:26
  53.5 9.1 %collective-permute-start.10 = (bf16[64,1792]{1,0:T(8,128)(2,1)S(1)}, bf16[64,1792]{1,0:T(8,128)(2,1)S(1)}, u32[]{:S(2)}, u32[]{:S(2)}) collective-permute-start(bf16[64,1792]{1,0:T(8,128)(2,1)S(1)} %shard_map.60), channel_id=1, source_target_pairs={{0,32},{1,481},{2,34},{3,483},{4,36},{5,485},{6,38},{7,487},{8,40}... | collective-permute-start | bytes 688136 | tf_op jit(solution)/shard_map/ppermute | solution.py:26
  59.1 7.2 %collective-permute-start.6 = (bf16[64,1792]{1,0:T(8,128)(2,1)S(1)}, bf16[64,1792]{1,0:T(8,128)(2,1)S(1)}, u32[]{:S(2)}, u32[]{:S(2)}) collective-permute-start(bf16[64,1792]{1,0:T(8,128)(2,1)S(1)} %shard_map.58), channel_id=1, source_target_pairs={{0,32},{1,481},{2,34},{3,483},{4,36},{5,485},{6,38},{7,487},{8,40}... | collective-permute-start | bytes 688136 | tf_op jit(solution)/shard_map/ppermute | solution.py:26
  62.7 8.0 %collective-permute-start.11 = (bf16[32,1792]{1,0:T(8,128)(2,1)S(1)}, bf16[32,1792]{1,0:T(8,128)(2,1)S(1)}, u32[]{:S(2)}, u32[]{:S(2)}) collective-permute-start(bf16[32,1792]{1,0:T(8,128)(2,1)S(1)} %get-tuple-element.40), channel_id=1, source_target_pairs={{0,64},{1,449},{2,66},{3,451},{4,68},{5,453},{6,70},{7,455},{8,72}... | collective-permute-start | bytes 344072 | tf_op jit(solution)/shard_map/ppermute | solution.py:26
  66.4 9.6 %collective-permute-start.7 = (bf16[32,1792]{1,0:T(8,128)(2,1)S(1)}, bf16[32,1792]{1,0:T(8,128)(2,1)S(1)}, u32[]{:S(2)}, u32[]{:S(2)}) collective-permute-start(bf16[32,1792]{1,0:T(8,128)(2,1)S(1)} %get-tuple-element.38), channel_id=1, source_target_pairs={{0,64},{1,449},{2,66},{3,451},{4,68},{5,453},{6,70},{7,455},{8,72}... | collective-permute-start | bytes 344072 | tf_op jit(solution)/shard_map/ppermute | solution.py:26
  70.8 9.7 %collective-permute-start.12 = (bf16[16,1792]{1,0:T(8,128)(2,1)S(1)}, bf16[16,1792]{1,0:T(8,128)(2,1)S(1)}, u32[]{:S(2)}, u32[]{:S(2)}) collective-permute-start(bf16[16,1792]{1,0:T(8,128)(2,1)S(1)} %fusion.2), channel_id=1, source_target_pairs={{0,128},{1,385},{2,130},{3,387},{4,132},{5,389},{6,134},{7,391},{8... | collective-permute-start | bytes 172040 | tf_op jit(solution)/shard_map/ppermute | solution.py:26
  80.5 16.7 %collective-permute-start.13 = (f32[16,1792]{1,0:T(8,128)S(1)}, f32[16,1792]{1,0:T(8,128)S(1)}, u32[]{:S(2)}, u32[]{:S(2)}) collective-permute-start(f32[16,1792]{1,0:T(8,128)S(1)} %fusion.3), channel_id=1, source_target_pairs={{0,33},{1,480},{2,35},{3,482},{4,37},{5,484},{6,39},{7,486},{8,41}... | collective-permute-start | bytes 344072 | tf_op jit(solution)/shard_map/ppermute | solution.py:26
  88.3 8.9 %collective-permute-start.8 = (bf16[16,1792]{1,0:T(8,128)(2,1)S(1)}, bf16[16,1792]{1,0:T(8,128)(2,1)S(1)}, u32[]{:S(2)}, u32[]{:S(2)}) collective-permute-start(bf16[16,1792]{1,0:T(8,128)(2,1)S(1)} %fusion.4), channel_id=1, source_target_pairs={{0,128},{1,385},{2,130},{3,387},{4,132},{5,389},{6,134},{7,391},{8... | collective-permute-start | bytes 172040 | tf_op jit(solution)/shard_map/ppermute | solution.py:26
where the time goes:
time: 98.4 us; the launch traced here: 97.9 us
  starting transfers between devices  66.5 us (68%)
  Pallas kernels  15.5 us (16%)
  waiting for transfers between devices  12.3 us (12%)
  local copies, waits for them, and re-layouts  2.22 us (2%)
  other arithmetic  1.05 us (1%)
    ppermute x14, starting transfers between devices, send(): return lax.ppermute(value, ('row', 'col'), joint(rule))  66.5 us
    ppermute x14, waiting for transfers between devices, send(): return lax.ppermute(value, ('row', 'col'), joint(rule))  12.3 us
    pallas_call x1, Pallas kernels, local_products(): pl.pallas_call(local_kernel, out_shape=(jax.ShapeDtypeStruct((4, 256, 115...  4.77 us
    pallas_call x1, Pallas kernels, halo_products(): pl.pallas_call(halo_kernel, out_shape=(jax.ShapeDtypeStruct((1024, 1280),...  3.15 us
    pallas_call x4, Pallas kernels, merged(): pl.pallas_call(merge_kernel, grid=(1,), out_shape=jax.ShapeDtypeStruct((6...  2.67 us
    pallas_call x1, Pallas kernels, place(): pl.pallas_call(place_kernel, out_shape=jax.ShapeDtypeStruct((1024, 768),...  2.26 us
  transfers between devices with their start and end apart: 14, of which 4 were waited for; matrix products, arithmetic and copies ran while one was open for 0% of the time, Pallas kernels for 11%

commit v1 on v0

--- a/solution.py
+++ b/solution.py
@@ -54,10 +54,11 @@
     return (((g >> 2) - pos_ref[2] + 33) & 31) * 4 + (g & 3)
 
 
-def pack(pos_ref, p_ref, out_ref, n, x, y):
+def pack(pos_ref, p_ref, out_ref, n, x, y, at_y=None):
+    at_y = y if at_y is None else at_y
     for t in range(3):
-        left = p_ref[(x * 4 + y) * 6 + 2 * t]
-        right = p_ref[(x * 4 + y) * 6 + 2 * t + 1]
+        left = p_ref[(x * 4 + at_y) * 6 + 2 * t]
+        right = p_ref[(x * 4 + at_y) * 6 + 2 * t + 1]
         at = 192 * n + 64 * t
         out_ref[at : at + 64, :] = jnp.concatenate([left, right], axis=1)
     row = lax.broadcasted_iota(jnp.int32, (16, 128), 0)
@@ -89,21 +90,39 @@
         store(slice(128 * m, 128 * m + 128), out)
 
 
-def pack_kernel(pos_ref, p_ref, cross_ref, chip_ref):
+def pack_kernel(pos_ref, p_ref, cross_ref, chip_ref, buf_ref, sems):
     core = pos_ref[0]
-    for x in range(4):
-        pack(pos_ref, p_ref, cross_ref, x, x, core * 3)
-        pack(pos_ref, p_ref, chip_ref, x, x, 3 - core * 3)
-
-
-def packed(kernel, pos, tiles):
+    copies = []
+    for side, y in enumerate((core * 3, 3 - core * 3)):
+        for x in range(4):
+            copies.append(
+                pltpu.make_async_copy(
+                    p_ref.at[pl.ds((x * 4 + y) * 6, 6)],
+                    buf_ref.at[pl.ds((x * 4 + side) * 6, 6)],
+                    sems.at[side * 4 + x],
+                )
+            )
+            copies[-1].start()
+    for side, (y, ref) in enumerate(((core * 3, cross_ref), (3 - core * 3, chip_ref))):
+        for x in range(4):
+            copies[side * 4 + x].wait()
+            pack(pos_ref, buf_ref, ref, x, x, y, side)
+
+
+def packed(kernel, pos, tiles, own_copies=False):
     return pl.pallas_call(
         kernel,
         out_shape=(jax.ShapeDtypeStruct((PART4, 128), BF16),) * 2,
-        in_specs=[smem(), vmem()],
+        in_specs=[smem(), pl.BlockSpec(memory_space=pltpu.HBM) if own_copies else vmem()],
         out_specs=(vmem(),) * 2,
+        scratch_shapes=[
+            pltpu.VMEM((96, B, B), BF16),
+            pltpu.SemaphoreType.DMA((8,)),
+        ]
+        if own_copies
+        else [],
         **budget(4, 0, 2000000),
-    )(pos, tiles)
+    )(pos, pltpu.with_memory_space_constraint(tiles, pltpu.HBM) if own_copies else tiles)
 
 
 def row_kernel(pos_ref, p_ref, up_ref, down_ref):
@@ -399,7 +418,7 @@
     pos = jnp.concatenate([jnp.stack([core, r, s]).astype(jnp.int32), coarse_blocks.reshape(96)])
 
     tiles = prolong_tiles.reshape(96, B, B)
-    cross, chip = packed(pack_kernel, pos, tiles)
+    cross, chip = packed(pack_kernel, pos, tiles, True)
     cross_in = send(cross, lambda r, s: (r, s - sign(s)))
     chip_in = send(chip, lambda r, s: (r, s + sign(s)))
     up_own, down_own = packed(row_kernel, pos, tiles)
@@ -452,6 +471,4 @@
         P("row", "col", None),
     )
     out_specs = P("col", "row", None)
-    return jax.shard_map(
-        body, mesh=mesh, in_specs=in_specs, out_specs=out_specs, check_vma=False
-    )
+    return jax.shard_map(body, mesh=mesh, in_specs=in_specs, out_specs=out_specs, check_vma=False)

time: 98.4 us -> 98.5 us (level)
  Pallas kernels: 15.5 us -> 16.9 us
  local copies, waits for them, and re-layouts: 2.22 us -> 0.93 us
    pallas_call x2, Pallas kernels: 1.49 us -> 2.91 us  [packed(): pl.pallas_call(kernel, out_shape=(jax.ShapeDtypeStruct((PART4, 128), BF16...]
    unnamed x10 -> x8, local copies, waits for them, and re-layouts: 1.43 us -> 0.02 us
where the time goes in v1:
time: 98.5 us; the launch traced here: 98 us
  starting transfers between devices  66.5 us (68%)
  Pallas kernels  16.9 us (17%)
  waiting for transfers between devices  12.2 us (12%)
  other arithmetic  1.05 us (1%)
    ppermute x14, starting transfers between devices, send(): return lax.ppermute(value, ('row', 'col'), joint(rule))  66.5 us
    ppermute x14, waiting for transfers between devices, send(): return lax.ppermute(value, ('row', 'col'), joint(rule))  12.2 us
    pallas_call x1, Pallas kernels, local_products(): pl.pallas_call(local_kernel, out_shape=(jax.ShapeDtypeStruct((4, 256, 115...  4.77 us
    pallas_call x1, Pallas kernels, halo_products(): pl.pallas_call(halo_kernel, out_shape=(jax.ShapeDtypeStruct((1024, 1280),...  3.15 us
    pallas_call x2, Pallas kernels, packed(): pl.pallas_call(kernel, out_shape=(jax.ShapeDtypeStruct((PART4, 128), BF16...  2.91 us
    pallas_call x4, Pallas kernels, merged(): pl.pallas_call(merge_kernel, grid=(1,), out_shape=jax.ShapeDtypeStruct((6...  2.67 us
    pallas_call x1, Pallas kernels, place(): pl.pallas_call(place_kernel, out_shape=jax.ShapeDtypeStruct((1024, 768),...  2.26 us
  transfers between devices with their start and end apart: 14, of which 4 were waited for; matrix products, arithmetic and copies ran while one was open for 0% of the time, Pallas kernels for 11%

profile of v1, /device:TPU:1, one launch (start us, length us, event | category | flops | bytes accessed | tf_op | source)
XLA Modules:
  0.0 98.0 jit_solution(17789131798385423023)
XLA Ops:
  0.0 0.9 reshape.9
  0.9 0.1 pad_add_fusion.pos_ref
  1.0 2.2 %shard_map.55 = (bf16[832,128]{1,0:T(8,128)(2,1)S(1)}, bf16[832,128]{1,0:T(8,128)(2,1)S(1)}) custom-call(s32[99]{0:T(128)S(1)} %pad_add_fusion.pos_ref, bf16[96,64,64]{2,1,0:T(8,128)(2,1)} %bitcast.7), custom_call_target="tpu_custom_call" | custom-call | bytes 2000000 | tf_op jit(solution)/shard_map/pallas_call | solution.py:113
  3.2 4.6 %collective-permute-start = (bf16[832,128]{1,0:T(8,128)(2,1)S(1)}, bf16[832,128]{1,0:T(8,128)(2,1)S(1)}, u32[]{:S(2)}, u32[]{:S(2)}) collective-permute-start(bf16[832,128]{1,0:T(8,128)(2,1)S(1)} %get-tuple-element.21), channel_id=1, source_target_pairs={{0,31},{1,2},{2,1},{3,4},{4,3},{5,6},{6,5},{7,8},{8,7},{9,10},{10,... | collective-permute-start | bytes 638984 | tf_op jit(solution)/shard_map/ppermute | solution.py:26
  7.8 6.1 %collective-permute-start.1 = (bf16[832,128]{1,0:T(8,128)(2,1)S(1)}, bf16[832,128]{1,0:T(8,128)(2,1)S(1)}, u32[]{:S(2)}, u32[]{:S(2)}) collective-permute-start(bf16[832,128]{1,0:T(8,128)(2,1)S(1)} %get-tuple-element.22), channel_id=1, source_target_pairs={{0,1},{1,0},{2,3},{3,2},{4,5},{5,4},{6,7},{7,6},{8,9},{9,8},{10,11... | collective-permute-start | bytes 638984 | tf_op jit(solution)/shard_map/ppermute | solution.py:26
  13.9 0.7 shard_map.56
  14.6 0.0 copy-start.1
  14.6 0.0 copy-start.2
  14.6 0.0 copy-start.3
  14.7 0.0 collective-permute-done.cross_ref
  14.7 0.3 collective-permute-done.1.chip_ref
  15.0 3.0 %collective-permute-start.2 = (bf16[1248,128]{1,0:T(8,128)(2,1)S(1)}, bf16[1248,128]{1,0:T(8,128)(2,1)S(1)}, u32[]{:S(2)}, u32[]{:S(2)}) collective-permute-start(bf16[1248,128]{1,0:T(8,128)(2,1)S(1)} %get-tuple-element.29), channel_id=1, source_target_pairs={{0,32},{1,33},{2,34},{3,35},{4,36},{5,37},{6,38},{7,39},{8,40},{9,... | collective-permute-start | bytes 958472 | tf_op jit(solution)/shard_map/ppermute | solution.py:26
  17.9 9.5 %collective-permute-start.3 = (bf16[1248,128]{1,0:T(8,128)(2,1)S(1)}, bf16[1248,128]{1,0:T(8,128)(2,1)S(1)}, u32[]{:S(2)}, u32[]{:S(2)}) collective-permute-start(bf16[1248,128]{1,0:T(8,128)(2,1)S(1)} %get-tuple-element.30), channel_id=1, source_target_pairs={{0,480},{1,481},{2,482},{3,483},{4,484},{5,485},{6,486},{7,487},{8... | collective-permute-start | bytes 958472 | tf_op jit(solution)/shard_map/ppermute | solution.py:26
  27.5 2.3 %place.1.po_ref = bf16[1024,768]{1,0:T(8,128)(2,1)S(1)} custom-call(s32[99]{0:T(128)S(1)} %pad_add_fusion.pos_ref, bf16[96,64,64]{2,1,0:T(8,128)(2,1)S(1)} %bitcast.9), custom_call_target="tpu_custom_call" | custom-call | bytes 2000000 | tf_op jit(solution)/shard_map/place/pallas_call | solution.py:155
  29.7 0.0 copy-done.1
  29.7 0.0 copy-done.2
  29.8 4.8 %local_products.1 = (bf16[4,256,1152]{2,1,0:T(8,128)(2,1)S(1)}, bf16[256,1024]{1,0:T(8,128)(2,1)S(1)}, bf16[512,1024]{1,0:T(8,128)(2,1)S(1)}, f32[1024,768]{1,0:T(8,128)S(1)}, bf16[2,256,768]{2,1,0:T(8,128)(2,1)S(1)}) custom-call(s32[99]{0:T(128)S(1)} %pad_add_fusion.pos_ref, s32[4,4,9]{2,1,0:T(4,128)S(1)} %copy-done.2, s32[4,4]{1,0:T(4,128)S(1)} %copy-done.3, ...), custom_call_target="tpu_custom_call" | custom-call | flops 1000000000 | bytes 12000000 | tf_op jit(solution)/shard_map/local_products/pallas_call | solution.py:268
  34.5 0.0 collective-permute-done.2.up_ref
  34.5 0.0 collective-permute-done.3.down_ref
  34.5 3.1 %halo_products.1 = (bf16[1024,1280]{1,0:T(8,128)(2,1)S(1)}, bf16[128,1280]{1,0:T(8,128)(2,1)S(1)}, bf16[128,1280]{1,0:T(8,128)(2,1)S(1)}) custom-call(s32[99]{0:T(128)S(1)} %pad_add_fusion.pos_ref, bf16[4,256,1152]{2,1,0:T(8,128)(2,1)S(1)} %get-tuple-element.23.ad_ref, bf16[256,1024]{1,0:T(8,128)(2,1)S(1)} %get-tuple-element.24.pt_ref, ...), custom_call_target="tpu_custom_call" | custom-call | flops 1500000000 | bytes 12000000 | tf_op jit(solution)/shard_map/halo_products/pallas_call | solution.py:342
  37.7 1.1 %own_pieces.1 = (f32[256,1280]{1,0:T(8,128)S(1)}, bf16[256,1280]{1,0:T(8,128)(2,1)S(1)}) custom-call(bf16[512,1024]{1,0:T(8,128)(2,1)S(1)} %get-tuple-element.32.pt_ref, bf16[1024,1280]{1,0:T(8,128)(2,1)S(1)} %get-tuple-element.33.im_ref), custom_call_target="tpu_custom_call" | custom-call | flops 1400000000 | bytes 6000000 | tf_op jit(solution)/shard_map/own_pieces/pallas_call | solution.py:363
  38.8 3.0 %collective-permute-start.5 = (bf16[256,1280]{1,0:T(8,128)(2,1)S(1)}, bf16[256,1280]{1,0:T(8,128)(2,1)S(1)}, u32[]{:S(2)}, u32[]{:S(2)}) collective-permute-start(bf16[256,1280]{1,0:T(8,128)(2,1)S(1)} %get-tuple-element.35), channel_id=1, source_target_pairs={{0,1},{1,0},{2,3},{3,2},{4,5},{5,4},{6,7},{7,6},{8,9},{9,8},{10,11... | collective-permute-start | bytes 1966088 | tf_op jit(solution)/shard_map/ppermute | solution.py:26
  41.8 1.9 %collective-permute-start.9 = (bf16[128,1280]{1,0:T(8,128)(2,1)S(1)}, bf16[128,1280]{1,0:T(8,128)(2,1)S(1)}, u32[]{:S(2)}, u32[]{:S(2)}) collective-permute-start(bf16[128,1280]{1,0:T(8,128)(2,1)S(1)} %get-tuple-element.36), channel_id=1, source_target_pairs={{0,30},{1,3},{2,0},{3,5},{4,2},{5,7},{6,4},{7,9},{8,6},{9,11},{10,... | collective-permute-start | bytes 983048 | tf_op jit(solution)/shard_map/ppermute | solution.py:26
  43.8 3.5 %collective-permute-start.4 = (bf16[128,1280]{1,0:T(8,128)(2,1)S(1)}, bf16[128,1280]{1,0:T(8,128)(2,1)S(1)}, u32[]{:S(2)}, u32[]{:S(2)}) collective-permute-start(bf16[128,1280]{1,0:T(8,128)(2,1)S(1)} %get-tuple-element.31), channel_id=1, source_target_pairs={{0,31},{1,2},{2,1},{3,4},{4,3},{5,6},{6,5},{7,8},{8,7},{9,10},{10,... | collective-permute-start | bytes 983048 | tf_op jit(solution)/shard_map/ppermute | solution.py:26
  47.3 5.7 %collective-permute-done.9.high_ref = bf16[128,1280]{1,0:T(8,128)(2,1)S(1)} collective-permute-done((bf16[128,1280]{1,0:T(8,128)(2,1)S(1)}, bf16[128,1280]{1,0:T(8,128)(2,1)S(1)}, u32[]{:S(2)}, u32[]{:S(2)}) %collective-permute-start.9) | collective-permute-done | bytes 327712 | tf_op jit(solution)/shard_map/ppermute | solution.py:26
  53.0 0.0 collective-permute-done.5.high_ref.middle_ref
  53.0 0.7 shard_map.60
  53.6 4.9 %collective-permute-start.10 = (bf16[64,1792]{1,0:T(8,128)(2,1)S(1)}, bf16[64,1792]{1,0:T(8,128)(2,1)S(1)}, u32[]{:S(2)}, u32[]{:S(2)}) collective-permute-start(bf16[64,1792]{1,0:T(8,128)(2,1)S(1)} %shard_map.60), channel_id=1, source_target_pairs={{0,32},{1,481},{2,34},{3,483},{4,36},{5,485},{6,38},{7,487},{8,40}... | collective-permute-start | bytes 688136 | tf_op jit(solution)/shard_map/ppermute | solution.py:26
  58.5 0.0 collective-permute-done.4.low_ref
  58.5 0.7 shard_map.58
  59.2 2.2 %collective-permute-start.6 = (bf16[64,1792]{1,0:T(8,128)(2,1)S(1)}, bf16[64,1792]{1,0:T(8,128)(2,1)S(1)}, u32[]{:S(2)}, u32[]{:S(2)}) collective-permute-start(bf16[64,1792]{1,0:T(8,128)(2,1)S(1)} %shard_map.58), channel_id=1, source_target_pairs={{0,32},{1,481},{2,34},{3,483},{4,36},{5,485},{6,38},{7,487},{8,40}... | collective-permute-start | bytes 688136 | tf_op jit(solution)/shard_map/ppermute | solution.py:26
  61.3 0.7 shard_map.59
  62.0 0.7 shard_map.57
  62.7 0.0 collective-permute-done.10
  62.7 0.1 slice_add_fusion.1
  62.8 3.6 %collective-permute-start.11 = (bf16[32,1792]{1,0:T(8,128)(2,1)S(1)}, bf16[32,1792]{1,0:T(8,128)(2,1)S(1)}, u32[]{:S(2)}, u32[]{:S(2)}) collective-permute-start(bf16[32,1792]{1,0:T(8,128)(2,1)S(1)} %get-tuple-element.40), channel_id=1, source_target_pairs={{0,64},{1,449},{2,66},{3,451},{4,68},{5,453},{6,70},{7,455},{8,72}... | collective-permute-start | bytes 344072 | tf_op jit(solution)/shard_map/ppermute | solution.py:26
  66.4 0.0 collective-permute-done.6
  66.4 0.1 slice_add_fusion.3
  66.5 4.3 %collective-permute-start.7 = (bf16[32,1792]{1,0:T(8,128)(2,1)S(1)}, bf16[32,1792]{1,0:T(8,128)(2,1)S(1)}, u32[]{:S(2)}, u32[]{:S(2)}) collective-permute-start(bf16[32,1792]{1,0:T(8,128)(2,1)S(1)} %get-tuple-element.38), channel_id=1, source_target_pairs={{0,64},{1,449},{2,66},{3,451},{4,68},{5,453},{6,70},{7,455},{8,72}... | collective-permute-start | bytes 344072 | tf_op jit(solution)/shard_map/ppermute | solution.py:26
  70.8 0.0 collective-permute-done.11
  70.9 5.2 %collective-permute-start.12 = (bf16[16,1792]{1,0:T(8,128)(2,1)S(1)}, bf16[16,1792]{1,0:T(8,128)(2,1)S(1)}, u32[]{:S(2)}, u32[]{:S(2)}) collective-permute-start(bf16[16,1792]{1,0:T(8,128)(2,1)S(1)} %fusion.2), channel_id=1, source_target_pairs={{0,128},{1,385},{2,130},{3,387},{4,132},{5,389},{6,134},{7,391},{8... | collective-permute-start | bytes 172040 | tf_op jit(solution)/shard_map/ppermute | solution.py:26
  76.1 0.0 collective-permute-done.7
  76.1 4.5 %collective-permute-done.12 = bf16[16,1792]{1,0:T(8,128)(2,1)S(1)} collective-permute-done((bf16[16,1792]{1,0:T(8,128)(2,1)S(1)}, bf16[16,1792]{1,0:T(8,128)(2,1)S(1)}, u32[]{:S(2)}, u32[]{:S(2)}) %collective-permute-start.12) | collective-permute-done | bytes 57376 | tf_op jit(solution)/shard_map/ppermute | solution.py:26
  80.6 7.7 %collective-permute-start.13 = (f32[16,1792]{1,0:T(8,128)S(1)}, f32[16,1792]{1,0:T(8,128)S(1)}, u32[]{:S(2)}, u32[]{:S(2)}) collective-permute-start(f32[16,1792]{1,0:T(8,128)S(1)} %fusion.3), channel_id=1, source_target_pairs={{0,33},{1,480},{2,35},{3,482},{4,37},{5,484},{6,39},{7,486},{8,41}... | collective-permute-start | bytes 344072 | tf_op jit(solution)/shard_map/ppermute | solution.py:26
  88.4 7.1 %collective-permute-start.8 = (bf16[16,1792]{1,0:T(8,128)(2,1)S(1)}, bf16[16,1792]{1,0:T(8,128)(2,1)S(1)}, u32[]{:S(2)}, u32[]{:S(2)}) collective-permute-start(bf16[16,1792]{1,0:T(8,128)(2,1)S(1)} %fusion.4), channel_id=1, source_target_pairs={{0,128},{1,385},{2,130},{3,387},{4,132},{5,389},{6,134},{7,391},{8... | collective-permute-start | bytes 172040 | tf_op jit(solution)/shard_map/ppermute | solution.py:26
  95.5 1.8 %collective-permute-done.8 = bf16[16,1792]{1,0:T(8,128)(2,1)S(1)} collective-permute-done((bf16[16,1792]{1,0:T(8,128)(2,1)S(1)}, bf16[16,1792]{1,0:T(8,128)(2,1)S(1)}, u32[]{:S(2)}, u32[]{:S(2)}) %collective-permute-start.8) | collective-permute-done | bytes 57376 | tf_op jit(solution)/shard_map/ppermute | solution.py:26
  97.3 0.0 collective-permute-done.13
  97.3 0.7 fusion.7
  (11 shorter events, 0.2 us)
Async XLA Ops:
  0.0 13.9 %copy-start = (bf16[4,4,6,64,64]{4,3,2,1,0:T(8,128)(2,1)S(1)}, bf16[4,4,6,64,64]{4,3,2,1,0:T(8,128)(2,1)}, u32[]{:S(2)}) copy-start(bf16[4,4,6,64,64]{4,3,2,1,0:T(8,128)(2,1)} %param.8) | copy-start | bytes 2359300
  3.2 11.5 %collective-permute-start = (bf16[832,128]{1,0:T(8,128)(2,1)S(1)}, bf16[832,128]{1,0:T(8,128)(2,1)S(1)}, u32[]{:S(2)}, u32[]{:S(2)}) collective-permute-start(bf16[832,128]{1,0:T(8,128)(2,1)S(1)} %get-tuple-element.21), channel_id=1, source_target_pairs={{0,31},{1,2},{2,1},{3,4},{4,3},{5,6},{6,5},{7,8},{8,7},{9,10},{10,... | collective-permute-start | bytes 638984 | tf_op jit(solution)/shard_map/ppermute | solution.py:26
  7.8 7.2 %collective-permute-start.1 = (bf16[832,128]{1,0:T(8,128)(2,1)S(1)}, bf16[832,128]{1,0:T(8,128)(2,1)S(1)}, u32[]{:S(2)}, u32[]{:S(2)}) collective-permute-start(bf16[832,128]{1,0:T(8,128)(2,1)S(1)} %get-tuple-element.22), channel_id=1, source_target_pairs={{0,1},{1,0},{2,3},{3,2},{4,5},{5,4},{6,7},{7,6},{8,9},{9,8},{10,11... | collective-permute-start | bytes 638984 | tf_op jit(solution)/shard_map/ppermute | solution.py:26
  14.6 15.1 %copy-start.1 = (bf16[4,4,9,64,64]{4,3,2,1,0:T(8,128)(2,1)S(1)}, bf16[4,4,9,64,64]{4,3,2,1,0:T(8,128)(2,1)}, u32[]{:S(2)}) copy-start(bf16[4,4,9,64,64]{4,3,2,1,0:T(8,128)(2,1)} %param.5) | copy-start | bytes 3538948
  14.6 15.1 %copy-start.2 = (s32[4,4,9]{2,1,0:T(4,128)S(1)}, s32[4,4,9]{2,1,0:T(4,128)}, u32[]{:S(2)}) copy-start(s32[4,4,9]{2,1,0:T(4,128)} %codes_ref.1) | copy-start | bytes 1732
  14.6 15.1 %copy-start.3 = (s32[4,4]{1,0:T(4,128)S(1)}, s32[4,4]{1,0:T(4,128)}, u32[]{:S(2)}) copy-start(s32[4,4]{1,0:T(4,128)} %live_ref.1) | copy-start | bytes 196
  15.0 19.6 %collective-permute-start.2 = (bf16[1248,128]{1,0:T(8,128)(2,1)S(1)}, bf16[1248,128]{1,0:T(8,128)(2,1)S(1)}, u32[]{:S(2)}, u32[]{:S(2)}) collective-permute-start(bf16[1248,128]{1,0:T(8,128)(2,1)S(1)} %get-tuple-element.29), channel_id=1, source_target_pairs={{0,32},{1,33},{2,34},{3,35},{4,36},{5,37},{6,38},{7,39},{8,40},{9,... | collective-permute-start | bytes 958472 | tf_op jit(solution)/shard_map/ppermute | solution.py:26
  17.9 16.6 %collective-permute-start.3 = (bf16[1248,128]{1,0:T(8,128)(2,1)S(1)}, bf16[1248,128]{1,0:T(8,128)(2,1)S(1)}, u32[]{:S(2)}, u32[]{:S(2)}) collective-permute-start(bf16[1248,128]{1,0:T(8,128)(2,1)S(1)} %get-tuple-element.30), channel_id=1, source_target_pairs={{0,480},{1,481},{2,482},{3,483},{4,484},{5,485},{6,486},{7,487},{8... | collective-permute-start | bytes 958472 | tf_op jit(solution)/shard_map/ppermute | solution.py:26
  38.8 14.1 %collective-permute-start.5 = (bf16[256,1280]{1,0:T(8,128)(2,1)S(1)}, bf16[256,1280]{1,0:T(8,128)(2,1)S(1)}, u32[]{:S(2)}, u32[]{:S(2)}) collective-permute-start(bf16[256,1280]{1,0:T(8,128)(2,1)S(1)} %get-tuple-element.35), channel_id=1, source_target_pairs={{0,1},{1,0},{2,3},{3,2},{4,5},{5,4},{6,7},{7,6},{8,9},{9,8},{10,11... | collective-permute-start | bytes 1966088 | tf_op jit(solution)/shard_map/ppermute | solution.py:26
  41.8 11.1 %collective-permute-start.9 = (bf16[128,1280]{1,0:T(8,128)(2,1)S(1)}, bf16[128,1280]{1,0:T(8,128)(2,1)S(1)}, u32[]{:S(2)}, u32[]{:S(2)}) collective-permute-start(bf16[128,1280]{1,0:T(8,128)(2,1)S(1)} %get-tuple-element.36), channel_id=1, source_target_pairs={{0,30},{1,3},{2,0},{3,5},{4,2},{5,7},{6,4},{7,9},{8,6},{9,11},{10,... | collective-permute-start | bytes 983048 | tf_op jit(solution)/shard_map/ppermute | solution.py:26
  43.8 14.8 %collective-permute-start.4 = (bf16[128,1280]{1,0:T(8,128)(2,1)S(1)}, bf16[128,1280]{1,0:T(8,128)(2,1)S(1)}, u32[]{:S(2)}, u32[]{:S(2)}) collective-permute-start(bf16[128,1280]{1,0:T(8,128)(2,1)S(1)} %get-tuple-element.31), channel_id=1, source_target_pairs={{0,31},{1,2},{2,1},{3,4},{4,3},{5,6},{6,5},{7,8},{8,7},{9,10},{10,... | collective-permute-start | bytes 983048 | tf_op jit(solution)/shard_map/ppermute | solution.py:26
  53.6 9.1 %collective-permute-start.10 = (bf16[64,1792]{1,0:T(8,128)(2,1)S(1)}, bf16[64,1792]{1,0:T(8,128)(2,1)S(1)}, u32[]{:S(2)}, u32[]{:S(2)}) collective-permute-start(bf16[64,1792]{1,0:T(8,128)(2,1)S(1)} %shard_map.60), channel_id=1, source_target_pairs={{0,32},{1,481},{2,34},{3,483},{4,36},{5,485},{6,38},{7,487},{8,40}... | collective-permute-start | bytes 688136 | tf_op jit(solution)/shard_map/ppermute | solution.py:26
  59.2 7.2 %collective-permute-start.6 = (bf16[64,1792]{1,0:T(8,128)(2,1)S(1)}, bf16[64,1792]{1,0:T(8,128)(2,1)S(1)}, u32[]{:S(2)}, u32[]{:S(2)}) collective-permute-start(bf16[64,1792]{1,0:T(8,128)(2,1)S(1)} %shard_map.58), channel_id=1, source_target_pairs={{0,32},{1,481},{2,34},{3,483},{4,36},{5,485},{6,38},{7,487},{8,40}... | collective-permute-start | bytes 688136 | tf_op jit(solution)/shard_map/ppermute | solution.py:26
  62.8 8.0 %collective-permute-start.11 = (bf16[32,1792]{1,0:T(8,128)(2,1)S(1)}, bf16[32,1792]{1,0:T(8,128)(2,1)S(1)}, u32[]{:S(2)}, u32[]{:S(2)}) collective-permute-start(bf16[32,1792]{1,0:T(8,128)(2,1)S(1)} %get-tuple-element.40), channel_id=1, source_target_pairs={{0,64},{1,449},{2,66},{3,451},{4,68},{5,453},{6,70},{7,455},{8,72}... | collective-permute-start | bytes 344072 | tf_op jit(solution)/shard_map/ppermute | solution.py:26
  66.5 9.6 %collective-permute-start.7 = (bf16[32,1792]{1,0:T(8,128)(2,1)S(1)}, bf16[32,1792]{1,0:T(8,128)(2,1)S(1)}, u32[]{:S(2)}, u32[]{:S(2)}) collective-permute-start(bf16[32,1792]{1,0:T(8,128)(2,1)S(1)} %get-tuple-element.38), channel_id=1, source_target_pairs={{0,64},{1,449},{2,66},{3,451},{4,68},{5,453},{6,70},{7,455},{8,72}... | collective-permute-start | bytes 344072 | tf_op jit(solution)/shard_map/ppermute | solution.py:26
  70.9 9.7 %collective-permute-start.12 = (bf16[16,1792]{1,0:T(8,128)(2,1)S(1)}, bf16[16,1792]{1,0:T(8,128)(2,1)S(1)}, u32[]{:S(2)}, u32[]{:S(2)}) collective-permute-start(bf16[16,1792]{1,0:T(8,128)(2,1)S(1)} %fusion.2), channel_id=1, source_target_pairs={{0,128},{1,385},{2,130},{3,387},{4,132},{5,389},{6,134},{7,391},{8... | collective-permute-start | bytes 172040 | tf_op jit(solution)/shard_map/ppermute | solution.py:26
  80.6 16.7 %collective-permute-start.13 = (f32[16,1792]{1,0:T(8,128)S(1)}, f32[16,1792]{1,0:T(8,128)S(1)}, u32[]{:S(2)}, u32[]{:S(2)}) collective-permute-start(f32[16,1792]{1,0:T(8,128)S(1)} %fusion.3), channel_id=1, source_target_pairs={{0,33},{1,480},{2,35},{3,482},{4,37},{5,484},{6,39},{7,486},{8,41}... | collective-permute-start | bytes 344072 | tf_op jit(solution)/shard_map/ppermute | solution.py:26
  88.4 8.9 %collective-permute-start.8 = (bf16[16,1792]{1,0:T(8,128)(2,1)S(1)}, bf16[16,1792]{1,0:T(8,128)(2,1)S(1)}, u32[]{:S(2)}, u32[]{:S(2)}) collective-permute-start(bf16[16,1792]{1,0:T(8,128)(2,1)S(1)} %fusion.4), channel_id=1, source_target_pairs={{0,128},{1,385},{2,130},{3,387},{4,132},{5,389},{6,134},{7,391},{8... | collective-permute-start | bytes 172040 | tf_op jit(solution)/shard_map/ppermute | solution.py:26
